TPU v7x, 1024 devices: a whole 4x4x32 slice. The times are simulated.
1024 devices in a mesh: wave: 32 (over x, y, core), lev: 32 (over z).
Axes of the slice: x: 4, y: 4, z: 32, core: 2. Of those that a mesh axis runs over, the one named last changes fastest.
Arguments:
- spectral: bfloat16 [2, 32, 2, 32, 1280], P(None, 'lev', None, 'wave'), may hold values from -6 to 6
- legendre: bfloat16 [32, 2560, 1280], P('wave'), may hold values from -0.15625 to 0.15625
- wavenumber: int32 [32], replicated, may hold values from 0 to 1279, as said below
Outputs:
- tendency_spec: bfloat16 [2, 32, 2, 32, 1280], P(None, 'lev', None, 'wave')
Inputs may be any that keep to these rules, and one draw needn't show every extreme that they name: `wavenumber`: distinct zonal wavenumbers; 0 and 1279 are always among them.
All inputs are finite; a program needn't handle non-finite values.
Results may differ from a plain program's by a relative error of at most 0.006.
Values may be sent and summed in bfloat16 or wider, within the bound.
A program may use at most 64 MiB of HBM per device.

v0:
```python
import math

import jax
import jax.numpy as jnp
from jax import lax
from jax.sharding import PartitionSpec as P


def circle_tables(latitude, band_index, wavenumber, lat_total, band_total, band_cap, wave_total):
    circle_length = 20 + 4 * jnp.minimum(latitude, lat_total - 1 - latitude)
    band_width = (circle_length + band_total - 1) // band_total
    offsets = jnp.arange(band_cap, dtype=jnp.int32)
    longitude_index = band_index[None, :, None] * band_width[:, None, None] + offsets[None, None, :]
    inside = (offsets[None, None, :] < band_width[:, None, None]) & (
        longitude_index < circle_length[:, None, None]
    )
    rows = latitude.shape[0]
    longitude_index = longitude_index.reshape(rows, -1)
    inside = inside.reshape(rows, -1)
    phase_index = (
        wavenumber[None, None, :] * longitude_index[:, :, None] % circle_length[:, None, None]
    )
    length_float = circle_length.astype(jnp.float32)
    angles = 2.0 * math.pi * phase_index.astype(jnp.float32) / length_float[:, None, None]
    shown = inside[:, :, None].astype(jnp.float32)
    trig_basis = jnp.stack([jnp.cos(angles) * shown, -jnp.sin(angles) * shown], axis=2)
    colatitude = (latitude.astype(jnp.float32) + 0.5) * (math.pi / lat_total)
    circle_weight = jnp.sin(colatitude) / jnp.sqrt(length_float)
    synth_table = (trig_basis / math.sqrt(wave_total)).astype(jnp.bfloat16)
    analysis_table = (trig_basis * circle_weight[:, None, None, None]).astype(jnp.bfloat16)
    return (synth_table, analysis_table, 2.0 * jnp.cos(colatitude))


def tendencies(grid_values, planetary):
    vorticity = grid_values[0]
    divergence = grid_values[1]
    absolute_vort = vorticity + planetary[None, :, None]
    column_div = jnp.sum(divergence, axis=0) / math.sqrt(divergence.shape[0])
    return jnp.stack(
        [-absolute_vort * divergence, absolute_vort * vorticity - divergence * column_div[None]]
    ).astype(jnp.bfloat16)


def body(spectral, legendre, wavenumber):
    wave_count = lax.axis_size("wave")
    lev_count = lax.axis_size("lev")
    wave_index = lax.axis_index("wave")
    lev_index = lax.axis_index("lev")
    lat_total = legendre.shape[1]
    degree_count = legendre.shape[2]
    set_span = lat_total // wave_count
    wave_total = wavenumber.shape[0]
    own_wave = lax.dynamic_slice_in_dim(wavenumber, wave_index, 1, 0)
    kept_degrees = (
        jnp.arange(degree_count, dtype=jnp.int32)[None, :] <= (degree_count - 1 - own_wave)[:, None]
    )
    masked_spec = jnp.where(kept_degrees, spectral, jnp.zeros_like(spectral))
    fourier = jnp.einsum(
        "flrsn,sjn->flrsj", masked_spec, legendre, preferred_element_type=jnp.float32
    ).astype(jnp.bfloat16)
    circle_max = 20 + 4 * (lat_total // 2 - 1)
    band_cap = (circle_max + lev_count - 1) // lev_count
    latitude = wave_index * set_span + jnp.arange(set_span, dtype=jnp.int32)
    band_index = jnp.reshape(lev_index, (1,))
    synth_table, analysis_table, planetary = circle_tables(
        latitude, band_index, wavenumber, lat_total, lev_count, band_cap, wave_total
    )
    level_fourier = lax.all_gather(fourier, "lev", axis=1, tiled=True)
    set_fourier = lax.all_to_all(level_fourier, "wave", split_axis=4, concat_axis=3, tiled=True)
    grid_values = jnp.einsum(
        "flrsq,qprs->flqp", set_fourier, synth_table, preferred_element_type=jnp.float32
    )
    tendency = tendencies(grid_values, planetary)
    summed = lax.psum_scatter(
        jnp.einsum(
            "flqp,qprs->lfrsq", tendency, analysis_table, preferred_element_type=jnp.float32
        ),
        "lev",
        scatter_dimension=0,
        tiled=True,
    )
    returned = lax.all_to_all(
        summed.astype(jnp.bfloat16), "wave", split_axis=3, concat_axis=4, tiled=True
    )
    analysed = jnp.einsum(
        "lfrsj,sjn->flrsn", returned, legendre, preferred_element_type=jnp.float32
    )
    return jnp.where(kept_degrees, analysed, jnp.zeros_like(analysed)).astype(jnp.bfloat16)


def solution(mesh):
    in_specs = (P(None, "lev", None, "wave", None), P("wave", None, None), P())
    out_specs = P(None, "lev", None, "wave", None)
    return jax.shard_map(body, mesh=mesh, in_specs=in_specs, out_specs=out_specs, check_vma=False)
```

profile of v0, /device:TPU:1, one launch (start us, length us, event | category | flops | bytes accessed | tf_op | source)
XLA Modules:
  0.0 313.1 jit_solution(7742904298087721067)
XLA Ops:
  6.5 1.2 dynamic_slice.3
  8.4 4.7 %fusion.7 = bf16[2,1,2,1,2560]{4,2,3,0,1:T(2,128)(2,1)S(1)} fusion(bf16[1,2560,1280]{2,1,0:T(8,128)(2,1)} %param.4, bf16[2,1,2,1,1280]{4,2,3,1,0:T(2,128)(2,1)} %param.3, pred[1280]{0:T(1024)(128)(4,1)S(1)} %iota_compare_fusion.1), kind=kOutput, calls=%fused_computation.11 | convolution fusion | flops 26229760 | bytes 6585600 | tf_op jit(solution)/shard_map/flrsn,sjn->flrsj/dot_general | solution.py:58
  13.2 58.5 %all_gather.3 = bf16[2,32,2,1,2560]{4,2,3,0,1:T(2,128)(2,1)S(1)} all-gather(bf16[2,1,2,1,2560]{4,2,3,0,1:T(2,128)(2,1)S(1)} %fusion.7), channel_id=1, replica_groups=mesh['wave'=32,'lev'=32] {'lev'}, dimensions={1}, use_global_device_ids=true | all-gather | bytes 675840 | tf_op jit(solution)/shard_map/all_gather | solution.py:68
  71.7 2.1 copy.24
  73.8 0.0 copy-start.1
  73.8 3.3 %reshape.254 = bf16[32,2,5120]{2,1,0:T(2,128)(2,1)} reshape(bf16[2560,2,1,2,32]{4,3,2,1,0:T(2,128)(2,1)S(1)} %bitcast.78) | data formatting | bytes 1310720
  77.1 21.6 %all-to-all-start = ((bf16[32,2,5120]{2,1,0:T(2,128)(2,1)}), bf16[32,2,5120]{2,1,0:T(2,128)(2,1)S(1)}, u32[]{:S(2)}, u32[]{:S(2)}) async-start(bf16[32,2,5120]{2,1,0:T(2,128)(2,1)} %reshape.254), calls=%async_computation | async-start | bytes 1310720 | tf_op jit(solution)/shard_map/all_to_all | solution.py:69
  98.6 0.2 reduce-scatter.2.cloned.1.call-start
  99.0 0.1 iota_add_fusion
  99.0 0.1 fusion.53
  99.2 0.0 copy-done.1
  99.2 36.6 %cosine_multiply_fusion = (f32[80,161,1,32]{1,3,2,0:T(8,128)S(1)}, f32[80,161,1,32]{1,3,2,0:T(8,128)}) fusion(f32[80,161]{1,0:T(8,128)S(1)} %fusion.53, f32[80]{0:T(128)S(1)} %fusion.63, pred[80]{0:T(512)(128)(4,1)S(1)} %broadcast_compare_fusion, s32[80]{0:T(128)S(1)} %get-tuple-element.9, s32[80,161]{1,0:T(8,128)S(1)} %iota_add_fusion, s32[32]{0:T(128)S(1)} %copy-done.1), kind=kLoop, calls=%fused_computation.30 | loop fusion | flops 5770240 | bytes 3401168 | tf_op jit(solution)/shard_map/mul | solution.py:26
  135.8 0.0 all-to-all-done
  135.8 2.3 reshape.255
  138.1 5.1 %fusion.35 = f32[2,32,80,161]{3,1,0,2:T(8,128)S(1)} fusion(bf16[2,32,2,32,80]{1,2,0,4,3:T(2,128)(2,1)} %bitcast.79, f32[80,161,1,32]{1,3,2,0:T(8,128)} %get-tuple-element.8, f32[80,161,1,32]{1,3,2,0:T(8,128)S(1)} %get-tuple-element.7), kind=kOutput, calls=%fused_computation.37 | convolution fusion | flops 107985920 | bytes 7249920 | tf_op jit(solution)/shard_map/flrsq,qprs->flqp/dot_general | solution.py:70
  143.2 0.4 slice_reduce_fusion
  143.6 0.0 copy-start
  143.6 0.7 fusion.11
  144.3 1.1 copy-done
  145.4 4.0 %fusion.32 = f32[32,2,2,32,80]{0,3,1,2,4:T(8,128)} fusion(bf16[1,32,80,161]{3,1,0,2:T(8,128)(2,1)S(1)} %get-tuple-element.6, bf16[1,32,80,161]{3,1,0,2:T(8,128)(2,1)S(1)} %get-tuple-element.5, f32[80,161,1,32]{1,3,2,0:T(8,128)S(1)} %copy-done, f32[80,161,1,32]{1,3,2,0:T(8,128)S(1)} %get-tuple-element.7, f32[80]{0:T(128)S(1)} %get-tuple-element.12), kind=kOutput, calls=%fused_computation.36 | convolution fusion | flops 111283200 | bytes 6256960 | tf_op jit(solution)/shard_map/flqp,qprs->lfrsq/dot_general | solution.py:75
  149.4 6.3 %copy.27 = f32[32,2,2,32,80]{4,3,2,1,0:T(8,128)} copy(f32[32,2,2,32,80]{0,3,1,2,4:T(8,128)} %fusion.32) | data formatting | bytes 2621440 | tf_op jit(solution)/shard_map/flqp,qprs->lfrsq/transpose | solution.py:75
  155.7 0.0 reduce-scatter.2.cloned.1.call-update
  155.7 108.1 %reduce-scatter.2.cloned.1.call-done = f32[1,2,2,32,80]{4,3,2,1,0:T(8,128)} async-done(((f32[32,2,2,32,80]{4,3,2,1,0:T(8,128)}), f32[1,2,2,32,80]{4,3,2,1,0:T(8,128)}) %reduce-scatter.2.cloned.1.call-update) | async-done | bytes 40976 | tf_op jit(solution)/shard_map/reduce_scatter | solution.py:74
  263.9 0.8 convert_element_type.82
  264.7 36.9 %all_to_all.21 = bf16[1,2,2,32,80]{4,2,1,0,3:T(2,128)(2,1)S(1)} all-to-all(bf16[1,2,2,32,80]{4,2,1,0,3:T(2,128)(2,1)S(1)} %copy.28), channel_id=1, replica_groups=mesh['wave'=32,'lev'=32] {'wave'}, dimensions={3} | all-to-all | bytes 40960 | tf_op jit(solution)/shard_map/all_to_all | solution.py:82
  301.7 0.1 reshape.248
  301.8 4.5 %fusion.49 = bf16[2,1,2,1,1280]{4,2,3,1,0:T(2,128)(2,1)} fusion(bf16[2,2,2560]{2,1,0:T(2,128)(2,1)S(1)} %reshape.248, bf16[1,2560,1280]{2,1,0:T(8,128)(2,1)} %param.4, pred[1280]{0:T(1024)(128)(4,1)S(1)} %iota_compare_fusion.1), kind=kOutput, calls=%fused_computation.42 | convolution fusion | flops 26224640 | bytes 6585600 | tf_op jit(solution)/shard_map/lfrsj,sjn->flrsn/dot_general | solution.py:85
  (9 shorter events, 0.2 us)
Async XLA Ops:
  73.8 25.4 %copy-start.1 = (s32[32]{0:T(128)S(1)}, s32[32]{0:T(128)}, u32[]{:S(2)}) copy-start(s32[32]{0:T(128)} %param.5) | copy-start | bytes 388
  77.1 58.7 %all-to-all-start = ((bf16[32,2,5120]{2,1,0:T(2,128)(2,1)}), bf16[32,2,5120]{2,1,0:T(2,128)(2,1)S(1)}, u32[]{:S(2)}, u32[]{:S(2)}) async-start(bf16[32,2,5120]{2,1,0:T(2,128)(2,1)} %reshape.254), calls=%async_computation | async-start | bytes 1310720 | tf_op jit(solution)/shard_map/all_to_all | solution.py:69
  98.6 165.2 %reduce-scatter.2.cloned.1.call-start = ((), (), s32[]{:S(2)}) async-start(), calls=%async_computation.3 | async-start | bytes 2162688 | tf_op jit(solution)/shard_map/reduce_scatter | solution.py:74
  143.6 1.7 copy-start
Sparse Core Ops, SparseCore 0:
  155.9 107.9 reduce-scatter.1
where the time goes:
time: 314 us; the launch traced here: 313 us
  waiting for transfers between devices  108 us (34%)
  blocking collectives  95.4 us (30%)
  other arithmetic  38.8 us (12%)
  starting transfers between devices  21.8 us (7%)
  matrix products  18.3 us (6%)
  local copies, waits for them, and re-layouts  16.4 us (5%)
  between operations  14.2 us (5%)
    reduce_scatter x1, waiting for transfers between devices, body(): lax.psum_scatter(jnp.einsum('flqp,qprs->lfrsq', tendency, analysis_table,...  108 us
    all_gather x1, blocking collectives, body(): level_fourier = lax.all_gather(fourier, 'lev', axis=1, tiled=True)  58.5 us
    all_to_all x1, blocking collectives, body(): lax.all_to_all(summed.astype(jnp.bfloat16), 'wave', split_axis=3, concat_...  36.9 us
    mul x1, other arithmetic, circle_tables(): jnp.cos(angles) * shown  36.6 us
    all_to_all x1, starting transfers between devices, body(): lax.all_to_all(level_fourier, 'wave', split_axis=4, concat_axis=3, tiled=...  21.6 us
    unnamed x6, local copies, waits for them, and re-layouts  6.62 us
    transpose x1, local copies, waits for them, and re-layouts, body(): jnp.einsum('flqp,qprs->lfrsq', tendency, analysis_table, preferred_elemen...  6.33 us
  transfers between devices with their start and end apart: 2, of which 1 were waited for; matrix products, arithmetic and copies ran while one was open for 12% of the time, Pallas kernels for 0%

commit v1 on v0

v1 whole, which is shorter than its diff:
```python
import math

import jax
import jax.numpy as jnp
from jax import lax
from jax.experimental import pallas as pl
from jax.experimental.pallas import tpu as pltpu
from jax.sharding import PartitionSpec as P

LATS = 2560
DEG = 1280
SETS = 32
SPAN = 80
LANES = 128
ROWS = (16, 24, 32, 40, 48)
F32 = jnp.float32
BF16 = jnp.bfloat16


def cos_turns(f):
    r = f - jnp.round(f)
    y = 0.25 - jnp.abs(r)
    z = y * y
    tau = 2.0 * math.pi
    coef = [(-1.0) ** k * tau ** (2 * k + 1) / math.factorial(2 * k + 1) for k in range(6)]
    acc = jnp.full_like(z, coef[5])
    for c in coef[4::-1]:
        acc = acc * z + c
    return acc * y


def turns(product, inv, length):
    q = jnp.round(product * inv)
    return (product - q * length) * inv


def fetch_copies(leg, table, sems):
    copies = []
    for w in range(SETS):
        for q in range(5):
            copies.append(
                pltpu.make_async_copy(
                    leg.at[q, w], table.at[w, 8 * q : 8 * q + 8], sems.at[w * 10 + q]
                )
            )
            copies.append(
                pltpu.make_async_copy(
                    leg.at[5 + q, SETS - 1 - w],
                    table.at[w, 40 + 8 * q : 48 + 8 * q],
                    sems.at[w * 10 + 5 + q],
                )
            )
    return copies


def forward_kernel(spec, leg, out, table, sems):
    copies = fetch_copies(leg, table, sems)
    for c in copies:
        c.start()
    rows = spec[...]
    for w in range(SETS):
        for c in copies[10 * w : 10 * w + 10]:
            c.wait()
        got = lax.dot_general(
            rows, table[w], (((1,), (1,)), ((), ())), preferred_element_type=F32
        )
        out[w, :, 0:SPAN] = got.astype(BF16)
        out[w, :, SPAN:] = jnp.zeros((8, LANES - SPAN), BF16)


def inverse_kernel(coef, leg, out, table, sems):
    copies = fetch_copies(leg, table, sems)
    for c in copies:
        c.start()
    acc = jnp.zeros((8, DEG), F32)
    for w in range(SETS):
        for c in copies[10 * w : 10 * w + 10]:
            c.wait()
        acc += jnp.dot(coef[w, :, 0:SPAN], table[w], preferred_element_type=F32)
    out[...] = acc


def grid_kernel(wave_f, fin, out, wide, lines, sums):
    me = lax.axis_index("wave")
    wide[...] = fin[...].astype(F32).reshape(SETS * 8, LANES)
    scale = 1.0 / math.sqrt(SETS)
    for k in range(3):
        re = wide[pl.ds(2 * k, SETS, stride=8), :] * scale
        im = wide[pl.ds(2 * k + 1, SETS, stride=8), :] * scale
        lines[k] = jnp.concatenate([re, im, -im, re], axis=0).T
    m_row = wave_f[...]
    m_lane = jnp.concatenate([m_row] * 4, axis=1)
    m_sub = jnp.broadcast_to(m_lane, (LANES, LANES)).T
    t_lane = lax.broadcasted_iota(jnp.int32, (64, LANES), 1).astype(F32)
    fine_base = m_sub[0:64] * t_lane
    fine_shift = jnp.where(
        lax.broadcasted_iota(jnp.int32, (64, LANES), 0) < SETS, 0.0, 0.25
    )

    def latitude(q, r, rows):
        n = 8 * q + r
        j = 256 * q + 8 * me + r
        length = jnp.full((8, LANES), 20 + 4 * j, jnp.int32).astype(F32)
        inv = 1.0 / length
        turn = (jnp.full((8, LANES), j, jnp.int32).astype(F32) + 0.5) / 5120.0
        planet = 2.0 * cos_turns(turn)[0:1]
        weight = (cos_turns(turn - 0.25) * lax.rsqrt(length))[0:1]
        length, inv = length[0:1], inv[0:1]
        fine = cos_turns(turns(fine_base, inv, length) + fine_shift).astype(BF16)
        fine = jnp.concatenate([fine, fine], axis=0)
        a_sub = lax.broadcasted_iota(jnp.int32, (rows, LANES), 0)
        lane = lax.broadcasted_iota(jnp.int32, (rows, LANES), 1)
        coarse_shift = jnp.where(lane < 64, 0.0, 0.25)
        coarse = cos_turns(
            turns((a_sub * LANES).astype(F32) * m_lane, inv, length) - coarse_shift
        )
        parts = []
        for k in range(3):
            for at in (n, 79 - n):
                parts.append(lines[k, pl.ds(at, 1), :] * coarse)
        left = jnp.concatenate(parts, axis=0).astype(BF16)
        grid = jnp.dot(left, fine, preferred_element_type=F32)
        inside = (a_sub * LANES + lane) < (20 + 4 * j)
        tend = []
        for h, sign in ((0, 1.0), (1, -1.0)):
            vort = grid[h * rows : (h + 1) * rows]
            div = grid[(2 + h) * rows : (3 + h) * rows]
            col = grid[(4 + h) * rows : (5 + h) * rows]
            total = vort + sign * planet
            tend.append((jnp.where(inside, -total * div, 0.0), jnp.where(inside, total * vort - div * col, 0.0)))
        right = jnp.concatenate([tend[0][0], tend[1][0], tend[0][1], tend[1][1]], axis=0)
        back = lax.dot_general(
            right.astype(BF16), fine, (((1,), (1,)), ((), ())), preferred_element_type=F32
        )
        for i in range(4):
            at = n if i % 2 == 0 else 79 - n
            line = jnp.sum(back[i * rows : (i + 1) * rows] * coarse, axis=0, keepdims=True)
            sums[i // 2, pl.ds(at, 1), :] = line * weight

    sums[...] = jnp.zeros_like(sums)
    for q in range(5):

        @pl.loop(0, 4)
        def _(step, q=q):
            for u in range(2):
                latitude(q, 2 * step + u, ROWS[q])

    for k in range(2):
        cols = sums[k].T
        wide[pl.ds(2 * k, SETS, stride=8), :] = cols[0:32] + cols[96:128]
        wide[pl.ds(2 * k + 1, SETS, stride=8), :] = cols[32:64] - cols[64:96]
        wide[pl.ds(2 * k + 4, SETS, stride=8), :] = jnp.zeros((SETS, LANES), F32)
        wide[pl.ds(2 * k + 5, SETS, stride=8), :] = jnp.zeros((SETS, LANES), F32)
    out[...] = wide[...].reshape(SETS, 8, LANES).astype(BF16)


def vmem():
    return pl.BlockSpec(memory_space=pltpu.VMEM)


def body(spectral, legendre, wavenumber):
    own = lax.dynamic_slice_in_dim(wavenumber, lax.axis_index("wave"), 1, 0)
    kept = jnp.arange(DEG, dtype=jnp.int32)[None, :] <= (DEG - 1 - own)[:, None]
    spec = spectral.reshape(4, DEG)
    spec = jnp.where(kept, spec, jnp.zeros_like(spec))
    column = lax.psum(spec[2:4].astype(F32), "lev") / math.sqrt(SETS)
    rows = jnp.concatenate([spec, column.astype(BF16), jnp.zeros((2, DEG), BF16)], axis=0)
    leg = legendre.reshape(10, SETS, 8, DEG)
    table = [pltpu.VMEM((SETS, SPAN, DEG), BF16), pltpu.SemaphoreType.DMA((SETS * 10,))]
    sent = pl.pallas_call(
        forward_kernel,
        out_shape=jax.ShapeDtypeStruct((SETS, 8, LANES), BF16),
        in_specs=[vmem(), pl.BlockSpec(memory_space=pl.ANY)],
        out_specs=vmem(),
        scratch_shapes=table,
    )(rows, leg)
    got = lax.all_to_all(sent, "wave", split_axis=0, concat_axis=0, tiled=True)
    tend = pl.pallas_call(
        grid_kernel,
        out_shape=jax.ShapeDtypeStruct((SETS, 8, LANES), BF16),
        in_specs=[vmem(), vmem()],
        out_specs=vmem(),
        scratch_shapes=[
            pltpu.VMEM((SETS * 8, LANES), F32),
            pltpu.VMEM((3, LANES, LANES), F32),
            pltpu.VMEM((2, LANES, LANES), F32),
        ],
    )(wavenumber.astype(F32)[None, :], got)
    back = lax.all_to_all(tend, "wave", split_axis=0, concat_axis=0, tiled=True)
    analysed = pl.pallas_call(
        inverse_kernel,
        out_shape=jax.ShapeDtypeStruct((8, DEG), F32),
        in_specs=[vmem(), pl.BlockSpec(memory_space=pl.ANY)],
        out_specs=vmem(),
        scratch_shapes=table,
    )(back, leg)[0:4]
    shown = jnp.where(kept, analysed, jnp.zeros_like(analysed)).astype(BF16)
    return shown.reshape(2, 1, 2, 1, DEG)


def solution(mesh):
    in_specs = (P(None, "lev", None, "wave", None), P("wave", None, None), P())
    out_specs = P(None, "lev", None, "wave", None)
    return jax.shard_map(body, mesh=mesh, in_specs=in_specs, out_specs=out_specs, check_vma=False)
```

time: 314 us -> 185 us (0.59)
  waiting for transfers between devices: 108 us -> 6.84 us
  other arithmetic: 38.8 us -> 2.01 us
  Pallas kernels: 0 us -> 30.1 us
  matrix products: 18.3 us -> 0 us
  between operations: 14.2 us -> 0.71 us
  starting transfers between devices: 21.8 us -> 35.2 us
  local copies, waits for them, and re-layouts: 16.4 us -> 3.33 us
  blocking collectives: 95.4 us -> 106 us
    reduce_scatter x1 -> x0, waiting for transfers between devices: 108 us -> none  [body(): lax.psum_scatter(jnp.einsum('flqp,qprs->lfrsq', tendency, analysis_table,...]
    psum x0 -> x1, blocking collectives: none -> 94.1 us  [body(): column = lax.psum(spec[2:4].astype(F32), 'lev') / math.sqrt(SETS)]
    all_gather x1 -> x0, blocking collectives: 58.5 us -> none  [body(): level_fourier = lax.all_gather(fourier, 'lev', axis=1, tiled=True)]
    mul x2 -> x0, other arithmetic: 36.7 us -> none  [the longest x1 36.6 us: circle_tables(): jnp.cos(angles) * shown]
    pallas_call x0 -> x3, Pallas kernels: none -> 30.1 us  [the longest x1 12.6 us: body(): pl.pallas_call(forward_kernel, out_shape=jax.ShapeDtypeStruct((SETS, 8, L...]
    all_to_all x1, blocking collectives: 36.9 us -> 12 us  [body(): back = lax.all_to_all(tend, 'wave', split_axis=0, concat_axis=0, tiled=True)]
    dot_general x4 -> x0, matrix products: 18.3 us -> none  [the longest x1 5.09 us: body(): jnp.einsum('flrsq,qprs->flqp', set_fourier, synth_table, preferred_elemen...]
    all_to_all x1, starting transfers between devices: 21.6 us -> 35.2 us  [body(): got = lax.all_to_all(sent, 'wave', split_axis=0, concat_axis=0, tiled=True)]
  transfers between devices with their start and end apart: 2 -> 1, of which waited for: 1 -> 1; matrix products, arithmetic and copies ran while one was open for 12% -> 0% of each run, Pallas kernels for 0% -> 0%
where the time goes in v1:
time: 185 us; the launch traced here: 184 us
  blocking collectives  106 us (57%)
  starting transfers between devices  35.2 us (19%)
  Pallas kernels  30.1 us (16%)
  waiting for transfers between devices  6.84 us (4%)
  local copies, waits for them, and re-layouts  3.33 us (2%)
  other arithmetic  2.01 us (1%)
    psum x1, blocking collectives, body(): column = lax.psum(spec[2:4].astype(F32), 'lev') / math.sqrt(SETS)  94.1 us
    all_to_all x1, starting transfers between devices, body(): got = lax.all_to_all(sent, 'wave', split_axis=0, concat_axis=0, tiled=True)  35.2 us
    pallas_call x1, Pallas kernels, body(): pl.pallas_call(forward_kernel, out_shape=jax.ShapeDtypeStruct((SETS, 8, L...  12.6 us
    all_to_all x1, blocking collectives, body(): back = lax.all_to_all(tend, 'wave', split_axis=0, concat_axis=0, tiled=True)  12 us
    pallas_call x1, Pallas kernels, body(): pl.pallas_call(grid_kernel, out_shape=jax.ShapeDtypeStruct((SETS, 8, LANE...  10.2 us
    pallas_call x1, Pallas kernels, body(): pl.pallas_call(inverse_kernel, out_shape=jax.ShapeDtypeStruct((8, DEG), F...  7.29 us
    all_to_all x1, waiting for transfers between devices, body(): got = lax.all_to_all(sent, 'wave', split_axis=0, concat_axis=0, tiled=True)  6.84 us
  transfers between devices with their start and end apart: 1, of which 1 were waited for; matrix products, arithmetic and copies ran while one was open for 0% of the time, Pallas kernels for 0%

profile of v1, /device:TPU:1, one launch (start us, length us, event | category | flops | bytes accessed | tf_op | source)
XLA Modules:
  0.0 184.3 jit_solution(36539337246129859)
XLA Ops:
  0.0 0.0 copy-start.1
  0.0 1.3 dynamic_slice.3
  2.0 0.7 reshape.17
  2.7 94.1 %psum.7 = f32[2,1280]{1,0:T(2,128)S(1)} all-reduce(f32[2,1280]{1,0:T(2,128)S(1)} %slice_convert_fusion), channel_id=1, replica_groups=mesh['wave'=32,'lev'=32] {'lev'}, use_global_device_ids=true, to_apply=%region_0.1 | all-reduce | flops 2560 | bytes 20480 | tf_op jit(solution)/shard_map/psum | solution.py:166
  96.8 0.1 pad.2.clone
  96.9 0.7 maximum_maximum_fusion.spec
  97.6 12.6 %shard_map.37 = bf16[32,8,128]{2,1,0:T(8,128)(2,1)} custom-call(bf16[8,1280]{1,0:T(8,128)(2,1)} %maximum_maximum_fusion.spec, bf16[10,32,8,1280]{3,2,1,0:T(8,128)(2,1)} %bitcast.7), custom_call_target="tpu_custom_call" | custom-call | tf_op jit(solution)/shard_map/pallas_call | solution.py:170
  110.2 35.2 %all-to-all-start = ((bf16[32,8,128]{2,1,0:T(8,128)(2,1)}), bf16[32,8,128]{2,1,0:T(8,128)(2,1)S(1)}, u32[]{:S(2)}, u32[]{:S(2)}) async-start(bf16[32,8,128]{2,1,0:T(8,128)(2,1)} %shard_map.37), calls=%async_computation | async-start | bytes 131072 | tf_op jit(solution)/shard_map/all_to_all | solution.py:177
  145.4 0.0 copy-done.1
  145.4 0.5 convert_bitcast_fusion.wave_f
  145.9 6.8 %all-to-all-done.fin = bf16[32,8,128]{2,1,0:T(8,128)(2,1)S(1)} async-done(((bf16[32,8,128]{2,1,0:T(8,128)(2,1)}), bf16[32,8,128]{2,1,0:T(8,128)(2,1)S(1)}, u32[]{:S(2)}, u32[]{:S(2)}) %all-to-all-start) | async-done | bytes 65568 | tf_op jit(solution)/shard_map/all_to_all | solution.py:177
  152.8 0.0 copy-start
  152.8 0.6 copy-done
  153.4 10.2 %shard_map.38 = bf16[32,8,128]{2,1,0:T(8,128)(2,1)} custom-call(f32[1,32]{1,0:T(1,128)} %convert_bitcast_fusion.wave_f, bf16[32,8,128]{2,1,0:T(8,128)(2,1)} %copy-done), custom_call_target="tpu_custom_call" | custom-call | tf_op jit(solution)/shard_map/pallas_call | solution.py:178
  163.6 12.0 %all_to_all.10.coef = bf16[32,8,128]{2,1,0:T(8,128)(2,1)} all-to-all(bf16[32,8,128]{2,1,0:T(8,128)(2,1)} %shard_map.38), channel_id=1, replica_groups=mesh['wave'=32,'lev'=32] {'wave'}, dimensions={0} | all-to-all | bytes 131072 | tf_op jit(solution)/shard_map/all_to_all | solution.py:189
  175.6 7.3 %shard_map.39 = f32[8,1280]{1,0:T(8,128)} custom-call(bf16[32,8,128]{2,1,0:T(8,128)(2,1)} %all_to_all.10.coef, bf16[10,32,8,1280]{3,2,1,0:T(8,128)(2,1)} %bitcast.8), custom_call_target="tpu_custom_call" | custom-call | tf_op jit(solution)/shard_map/pallas_call | solution.py:190
  182.9 0.8 fusion
  183.7 0.6 reshape.19
  (5 shorter events, 0.0 us)
Async XLA Ops:
  0.0 145.4 %copy-start.1 = (s32[32]{0:T(128)S(1)}, s32[32]{0:T(128)}, u32[]{:S(2)}) copy-start(s32[32]{0:T(128)} %param.5) | copy-start | bytes 388
  110.2 42.6 %all-to-all-start = ((bf16[32,8,128]{2,1,0:T(8,128)(2,1)}), bf16[32,8,128]{2,1,0:T(8,128)(2,1)S(1)}, u32[]{:S(2)}, u32[]{:S(2)}) async-start(bf16[32,8,128]{2,1,0:T(8,128)(2,1)} %shard_map.37), calls=%async_computation | async-start | bytes 131072 | tf_op jit(solution)/shard_map/all_to_all | solution.py:177
  152.8 0.6 copy-start

commit v2 on v0

v2 whole, which is shorter than its diff:
```python
import functools
import math

import jax
import jax.numpy as jnp
from jax import lax
from jax.experimental import pallas as pl
from jax.experimental.pallas import tpu as pltpu
from jax.sharding import PartitionSpec as P

LATS = 2560
DEG = 1280
SETS = 32
LEVELS = 32
LANES = 128
HOP = 2
NODES = LEVELS // HOP
RIGHT = NODES // 2
LEFT = NODES - 1 - RIGHT
ROWS = (16, 24, 32, 40, 48)
F32 = jnp.float32
BF16 = jnp.bfloat16
MESH = pl.DeviceIdType.MESH


def cos_turns(f):
    r = f - jnp.round(f)
    y = 0.25 - jnp.abs(r)
    z = y * y
    tau = 2.0 * math.pi
    coef = [(-1.0) ** k * tau ** (2 * k + 1) / math.factorial(2 * k + 1) for k in range(6)]
    acc = jnp.full_like(z, coef[5])
    for c in coef[4::-1]:
        acc = acc * z + c
    return acc * y


def turns(product, inv, length):
    q = jnp.round(product * inv)
    return (product - q * length) * inv


def kernel(spec, waves, leg, out, *scratch):
    (table, table_sem, xt, zs, sends, gets, wide, lines, sums, fine_s, pair_s, deg_s) = scratch[:12]
    coarse_s = scratch[12:17]
    grid_s = scratch[17:22]
    (own_s, near_s, node_s, right_s, left_s, near_sem, right_sem, left_sem, plane_sem) = scratch[22:]
    me = lax.axis_index("wave")
    lev = lax.axis_index("lev")

    loads = [
        pltpu.make_async_copy(
            leg.at[pl.ds(256 * q, 256)], table.at[pl.ds(256 * q, 256)], table_sem.at[q]
        )
        for q in range(10)
    ]
    for c in loads:
        c.start()

    barrier = pltpu.get_barrier_semaphore()

    def greet(d, _):
        pl.semaphore_signal(
            barrier, inc=1, device_id=(lax.rem(me + d, SETS), lev), device_id_type=MESH
        )
        return 0

    z_peers = sorted({1, LEVELS - 1, HOP, LEVELS - HOP})
    for d in z_peers:
        pl.semaphore_signal(
            barrier, inc=1, device_id=(me, lax.rem(lev + d, LEVELS)), device_id_type=MESH
        )
    lax.fori_loop(1, SETS, greet, 0)

    m_lane = jnp.concatenate([waves[...].astype(F32)] * 4, axis=1)
    m_sub = jnp.broadcast_to(m_lane, (LANES, LANES)).T
    lane8 = lax.broadcasted_iota(jnp.int32, (8, LANES), 1)
    own_m = jnp.sum(jnp.where(lane8[0:1, 0:SETS] == me, m_lane[:, 0:SETS], 0.0), axis=1, keepdims=True)
    degree = lax.broadcasted_iota(jnp.int32, (4, DEG), 1).astype(F32)
    kept = degree <= (DEG - 1.0) - own_m
    rows = jnp.concatenate([spec[0].astype(F32), spec[1].astype(F32)], axis=0)
    rows = jnp.where(kept, rows, 0.0)
    own_s[...] = rows[2:4].astype(BF16)
    group_of = lane8 // 8
    group_masks = [group_of == g for g in range(16)]

    def set_right(x):
        block = jnp.concatenate([x, jnp.zeros((8 - x.shape[0], DEG), F32)], axis=0)
        block = jnp.concatenate([block] * 16, axis=0)
        for k in range(10):
            xt[LANES * k : LANES * (k + 1), :] = block[:, LANES * k : LANES * (k + 1)].T.astype(BF16)

    def product(q):
        got = jnp.dot(table[256 * q : 256 * q + 256, :], xt[...], preferred_element_type=F32)
        for b in range(2):
            acc = jnp.zeros((8, LANES), F32)
            for g in range(16):
                w = 16 * b + g
                w = w if q < 5 else SETS - 1 - w
                acc = jnp.where(group_masks[g], got[8 * w : 8 * w + 8], acc)
            zs[b, 8 * q : 8 * q + 8, :] = acc

    def post(stage):
        for b in range(2):
            sends[stage, 16 * b : 16 * b + 16] = zs[b].T.reshape(16, 8, LANES).astype(BF16)

    def plane_copy(stage, d):
        to = lax.rem(me + d, SETS)
        return pltpu.make_async_remote_copy(
            src_ref=sends.at[stage, to],
            dst_ref=gets.at[stage, me],
            send_sem=plane_sem.at[stage, 0, d],
            recv_sem=plane_sem.at[stage, 1, d],
            device_id=(to, lev),
            device_id_type=MESH,
        )

    def plane_start(stage):
        def one(d, _):
            plane_copy(stage, d).start()
            return 0

        lax.fori_loop(1, SETS, one, 0)
        gets[stage, me] = sends[stage, me]

    def plane_wait(stage):
        def one(d, _):
            origin = lax.rem(me - d + SETS, SETS)
            pltpu.make_async_remote_copy(
                src_ref=sends.at[stage, lax.rem(me + d, SETS)],
                dst_ref=gets.at[stage, origin],
                send_sem=plane_sem.at[stage, 0, d],
                recv_sem=plane_sem.at[stage, 1, d],
                device_id=(origin, lev),
                device_id_type=MESH,
            ).wait()
            return 0

        lax.fori_loop(1, SETS, one, 0)

    def z_copy(src, dst, sems, i, shift):
        return pltpu.make_async_remote_copy(
            src_ref=src,
            dst_ref=dst,
            send_sem=sems.at[0, i],
            recv_sem=sems.at[1, i],
            device_id=(me, lax.rem(lev + shift, LEVELS)),
            device_id_type=MESH,
        )

    near = z_copy(own_s, near_s, near_sem, 0, LEVELS - 1)
    rights = [
        z_copy(node_s if s == 0 else right_s.at[s - 1], right_s.at[s], right_sem, s, HOP)
        for s in range(RIGHT)
    ]
    lefts = [
        z_copy(node_s if s == 0 else left_s.at[s - 1], left_s.at[s], left_sem, s, LEVELS - HOP)
        for s in range(LEFT)
    ]

    def ring(s):
        if s < RIGHT:
            rights[s].wait_recv()
            if s + 1 < RIGHT:
                rights[s + 1].start()
        if s < LEFT:
            lefts[s].wait_recv()
            if s + 1 < LEFT:
                lefts[s + 1].start()

    t_lane = lax.broadcasted_iota(jnp.int32, (64, LANES), 1).astype(F32)

    def tables(q):
        a_sub = lax.broadcasted_iota(jnp.int32, (ROWS[q], LANES), 0)
        lane = lax.broadcasted_iota(jnp.int32, (ROWS[q], LANES), 1)
        coarse_base = (a_sub * LANES).astype(F32) * m_lane
        coarse_shift = jnp.where(lane < 64, 0.0, 0.25)
        fine_base = m_sub[0:64] * t_lane
        fine_shift = jnp.where(lax.broadcasted_iota(jnp.int32, (64, LANES), 0) < SETS, 0.0, 0.25)

        def one(r, _):
            n = 8 * q + r
            j = 256 * q + 8 * me + r
            length = jnp.full((8, LANES), 20 + 4 * j, jnp.int32).astype(F32)
            inv = 1.0 / length
            turn = (jnp.full((8, LANES), j, jnp.int32).astype(F32) + 0.5) / 5120.0
            planet = 2.0 * cos_turns(turn)
            weight = cos_turns(turn - 0.25) * lax.rsqrt(length)
            pair_s[n, 0] = planet
            pair_s[n, 1] = weight
            length, inv = length[0:1], inv[0:1]
            fine = cos_turns(turns(fine_base, inv, length) + fine_shift).astype(BF16)
            fine_s[n, 0:64] = fine
            fine_s[n, 64:128] = fine
            coarse_s[q][r] = cos_turns(turns(coarse_base, inv, length) - coarse_shift)
            return 0

        lax.fori_loop(0, 8, one, 0, unroll=2)

    scale = 1.0 / math.sqrt(LEVELS)

    def take_lines(stage, count, base):
        wide[...] = gets[stage].astype(F32).reshape(SETS * 8, LANES)
        for k in range(count):
            re = wide[pl.ds(2 * k, SETS, stride=8), :] * scale
            im = wide[pl.ds(2 * k + 1, SETS, stride=8), :] * scale
            lines[base + k] = jnp.concatenate([re, im, -im, re], axis=0).T

    def synth(q):
        def one(r, _):
            n = 8 * q + r
            coarse = coarse_s[q][r]
            parts = [
                lines[k, pl.ds(at, 1), :] * coarse for k in range(2) for at in (n, 79 - n)
            ]
            left = jnp.concatenate(parts, axis=0).astype(BF16)
            grid_s[q][r] = jnp.dot(left, fine_s[n], preferred_element_type=F32)
            return 0

        lax.fori_loop(0, 8, one, 0, unroll=2)

    def finish(q):
        count = ROWS[q]
        a_sub = lax.broadcasted_iota(jnp.int32, (count, LANES), 0)
        lane = lax.broadcasted_iota(jnp.int32, (count, LANES), 1)
        point = a_sub * LANES + lane

        def one(r, _):
            n = 8 * q + r
            j = 256 * q + 8 * me + r
            coarse = coarse_s[q][r]
            fine = fine_s[n]
            planet = pair_s[n, 0, 0:1]
            weight = pair_s[n, 1, 0:1]
            left = jnp.concatenate(
                [lines[2, pl.ds(at, 1), :] * coarse for at in (n, 79 - n)], axis=0
            ).astype(BF16)
            col = jnp.dot(left, fine, preferred_element_type=F32)
            inside = point < (20 + 4 * j)
            first, second = [], []
            for h, sign in ((0, 1.0), (1, -1.0)):
                vort = grid_s[q][r, h * count : (h + 1) * count]
                div = grid_s[q][r, (2 + h) * count : (3 + h) * count]
                total = vort + sign * planet
                first.append(jnp.where(inside, -total * div, 0.0))
                second.append(
                    jnp.where(inside, total * vort - div * col[h * count : (h + 1) * count], 0.0)
                )
            tend = jnp.concatenate(first + second, axis=0).astype(BF16)
            back = lax.dot_general(
                tend, fine, (((1,), (1,)), ((), ())), preferred_element_type=F32
            )
            for i in range(4):
                at = n if i % 2 == 0 else 79 - n
                line = jnp.sum(back[i * count : (i + 1) * count] * coarse, axis=0, keepdims=True)
                sums[i // 2, pl.ds(at, 1), :] = line * weight
            return 0

        lax.fori_loop(0, 8, one, 0, unroll=4)

    set_right(rows)
    zs[...] = jnp.zeros_like(zs)
    sums[...] = jnp.zeros_like(sums)
    pl.semaphore_wait(barrier, SETS - 1 + len(z_peers))
    near.start()
    for q in range(5):
        loads[q].wait()
        product(q)
    near.wait_recv()
    node_s[...] = (rows[2:4] + near_s[...].astype(F32)).astype(BF16)
    for q in range(5, 7):
        loads[q].wait()
        product(q)
    rights[0].start()
    lefts[0].start()
    for q in range(7, 10):
        loads[q].wait()
        product(q)
    post(0)
    ring(0)
    tables(0)
    plane_start(0)
    tables(1)
    ring(1)
    tables(2)
    tables(3)
    ring(2)
    tables(4)
    plane_wait(0)
    take_lines(0, 2, 0)
    ring(3)
    synth(0)
    synth(1)
    ring(4)
    synth(2)
    ring(5)
    synth(3)
    ring(6)
    synth(4)
    for s in range(7, max(RIGHT, LEFT)):
        ring(s)
    total = node_s[...].astype(F32)
    for s in range(RIGHT):
        total += right_s[s].astype(F32)
    for s in range(LEFT):
        total += left_s[s].astype(F32)
    set_right(total * scale)
    for q in range(10):
        product(q)
    post(1)
    near.wait_send()
    for c in rights + lefts:
        c.wait_send()
    plane_start(1)
    plane_wait(1)
    take_lines(1, 1, 2)
    for q in range(5):
        finish(q)
    for k in range(2):
        cols = sums[k].T
        wide[pl.ds(2 * k, SETS, stride=8), :] = cols[0:32] + cols[96:128]
        wide[pl.ds(2 * k + 1, SETS, stride=8), :] = cols[32:64] - cols[64:96]
        wide[pl.ds(2 * k + 4, SETS, stride=8), :] = jnp.zeros((SETS, LANES), F32)
        wide[pl.ds(2 * k + 5, SETS, stride=8), :] = jnp.zeros((SETS, LANES), F32)
    sends[2] = wide[...].reshape(SETS, 8, LANES).astype(BF16)
    plane_start(2)
    plane_wait(2)
    wide[...] = gets[2].astype(F32).reshape(SETS * 8, LANES)
    for q in range(10):
        for b in range(2):
            acc = jnp.zeros((8, LANES), F32)
            for g in range(16):
                w = 16 * b + g
                w = w if q < 5 else SETS - 1 - w
                piece = pltpu.roll(wide[8 * w : 8 * w + 8, :], (8 * g - 8 * q) % LANES, 1)
                acc = jnp.where(group_masks[g], piece, acc)
            deg_s[:, 256 * q + LANES * b : 256 * q + LANES * (b + 1)] = acc
    result = jnp.dot(deg_s[...].astype(BF16), table[...], preferred_element_type=F32)[0:4]
    result = jnp.where(kept, result, 0.0)
    out[0] = result[0:2].astype(BF16)
    out[1] = result[2:4].astype(BF16)


def body(spectral, legendre, wavenumber):
    anywhere = pl.BlockSpec(memory_space=pl.ANY)
    local = pl.BlockSpec(memory_space=pltpu.VMEM)
    dma = pltpu.SemaphoreType.DMA
    scratch = [
        pltpu.VMEM((LATS, DEG), BF16),
        dma((10,)),
        pltpu.VMEM((DEG, LANES), BF16),
        pltpu.VMEM((2, LANES, LANES), F32),
        pltpu.VMEM((3, SETS, 8, LANES), BF16),
        pltpu.VMEM((3, SETS, 8, LANES), BF16),
        pltpu.VMEM((SETS * 8, LANES), F32),
        pltpu.VMEM((3, LANES, LANES), F32),
        pltpu.VMEM((2, LANES, LANES), F32),
        pltpu.VMEM((40, LANES, LANES), BF16),
        pltpu.VMEM((40, 2, 8, LANES), F32),
        pltpu.VMEM((8, LATS), F32),
    ]
    scratch += [pltpu.VMEM((8, n, LANES), F32) for n in ROWS]
    scratch += [pltpu.VMEM((8, 4 * n, LANES), F32) for n in ROWS]
    scratch += [
        pltpu.VMEM((2, DEG), BF16),
        pltpu.VMEM((2, DEG), BF16),
        pltpu.VMEM((2, DEG), BF16),
        pltpu.VMEM((RIGHT, 2, DEG), BF16),
        pltpu.VMEM((LEFT, 2, DEG), BF16),
        dma((2, 1)),
        dma((2, RIGHT)),
        dma((2, LEFT)),
        dma((3, 2, SETS)),
    ]
    result = pl.pallas_call(
        kernel,
        out_shape=jax.ShapeDtypeStruct((2, 2, DEG), BF16),
        in_specs=[local, local, anywhere],
        out_specs=local,
        scratch_shapes=scratch,
        compiler_params=pltpu.CompilerParams(
            collective_id=0, has_side_effects=True, vmem_limit_bytes=48 * 1024 * 1024
        ),
    )(spectral.reshape(2, 2, DEG), wavenumber.reshape(1, SETS), legendre.reshape(LATS, DEG))
    return result.reshape(2, 1, 2, 1, DEG)


def solution(mesh):
    in_specs = (P(None, "lev", None, "wave", None), P("wave", None, None), P())
    out_specs = P(None, "lev", None, "wave", None)
    return jax.shard_map(body, mesh=mesh, in_specs=in_specs, out_specs=out_specs, check_vma=False)
```

time: 314 us -> 76.7 us (0.24)
  waiting for transfers between devices: 108 us -> 0 us
  blocking collectives: 95.4 us -> 0 us
  Pallas kernels: 0 us -> 74.6 us
  other arithmetic: 38.8 us -> 0 us
  starting transfers between devices: 21.8 us -> 0 us
  matrix products: 18.3 us -> 0 us
  local copies, waits for them, and re-layouts: 16.4 us -> 1.96 us
  between operations: 14.2 us -> 0.01 us
    reduce_scatter x1 -> x0, waiting for transfers between devices: 108 us -> none  [body(): lax.psum_scatter(jnp.einsum('flqp,qprs->lfrsq', tendency, analysis_table,...]
    pallas_call x0 -> x1, Pallas kernels: none -> 74.6 us  [body(): pl.pallas_call(kernel, out_shape=jax.ShapeDtypeStruct((2, 2, DEG), BF16),...]
    all_gather x1 -> x0, blocking collectives: 58.5 us -> none  [body(): level_fourier = lax.all_gather(fourier, 'lev', axis=1, tiled=True)]
    all_to_all x1 -> x0, blocking collectives: 36.9 us -> none  [body(): lax.all_to_all(summed.astype(jnp.bfloat16), 'wave', split_axis=3, concat_...]
    mul x2 -> x0, other arithmetic: 36.7 us -> none  [the longest x1 36.6 us: circle_tables(): jnp.cos(angles) * shown]
    all_to_all x1 -> x0, starting transfers between devices: 21.6 us -> none  [body(): lax.all_to_all(level_fourier, 'wave', split_axis=4, concat_axis=3, tiled=...]
    dot_general x4 -> x0, matrix products: 18.3 us -> none  [the longest x1 5.09 us: body(): jnp.einsum('flrsq,qprs->flqp', set_fourier, synth_table, preferred_elemen...]
    transpose x1 -> x0, local copies, waits for them, and re-layouts: 6.33 us -> none  [body(): jnp.einsum('flqp,qprs->lfrsq', tendency, analysis_table, preferred_elemen...]
  transfers between devices with their start and end apart: 2 -> 0, of which waited for: 1 -> 0; matrix products, arithmetic and copies ran while one was open for 12% -> 0% of each run, Pallas kernels for 0% -> 0%
where the time goes in v2:
time: 76.7 us; the launch traced here: 76.5 us
  Pallas kernels  74.6 us (97%)
  local copies, waits for them, and re-layouts  1.96 us (3%)
    pallas_call x1, Pallas kernels, body(): pl.pallas_call(kernel, out_shape=jax.ShapeDtypeStruct((2, 2, DEG), BF16),...  74.6 us
    unnamed x5, local copies, waits for them, and re-layouts  1.96 us

profile of v2, /device:TPU:1, one launch (start us, length us, event | category | flops | bytes accessed | tf_op | source)
XLA Modules:
  0.0 76.5 jit_solution(6131414184493250775)
XLA Ops:
  0.0 0.0 copy-start
  0.0 0.7 copy-done
  0.7 0.0 copy-start.1
  0.7 0.7 copy-done.1
  1.4 74.6 %shard_map.37 = bf16[2,2,1280]{2,1,0:T(2,128)(2,1)S(1)} custom-call(bf16[2,2,1280]{2,1,0:T(2,128)(2,1)S(1)} %bitcast.7, s32[1,32]{1,0:T(1,128)S(1)} %bitcast.8, bf16[2560,1280]{1,0:T(8,128)(2,1)} %bitcast.9), custom_call_target="tpu_custom_call" | custom-call | tf_op jit(solution)/shard_map/pallas_call | solution.py:375
  75.9 0.6 copy.6
Async XLA Ops:
  0.0 0.7 copy-start
  0.7 0.7 copy-start.1

commit v3 on v2

v3 whole, which is shorter than its diff:
```python
import functools
import math

import jax
import jax.numpy as jnp
from jax import lax
from jax.experimental import pallas as pl
from jax.experimental.pallas import tpu as pltpu
from jax.sharding import PartitionSpec as P

LATS = 2560
DEG = 1280
SETS = 32
LEVELS = 32
LANES = 128
HOP = 8
NODES = LEVELS // HOP
RIGHT = NODES // 2
NEAR = [o for o in range(1 - HOP // 2, HOP // 2 + 1) if o] if HOP > 1 else []
LEFT = NODES - 1 - RIGHT
FINISH = 4
ROWS = (16, 24, 32, 40, 48)
F32 = jnp.float32
BF16 = jnp.bfloat16
MESH = pl.DeviceIdType.MESH


def cos_turns(f):
    r = f - jnp.round(f)
    y = 0.25 - jnp.abs(r)
    z = y * y
    tau = 2.0 * math.pi
    coef = [(-1.0) ** k * tau ** (2 * k + 1) / math.factorial(2 * k + 1) for k in range(6)]
    acc = jnp.full_like(z, coef[5])
    for c in coef[4::-1]:
        acc = acc * z + c
    return acc * y


def turns(product, inv, length):
    q = jnp.round(product * inv)
    return (product - q * length) * inv


def kernel(spec_in, waves_in, leg, out, *scratch):
    (spec, waves, in_sem, table, table_sem, sends, gets, wide, lines, sums, fine_s, pair_s, nat_s) = scratch[:13]
    coarse_s = scratch[13:18]
    grid_s = scratch[18:23]
    (own_s, near_s, node_s, total_s, right_s, left_s, near_sem, right_sem, left_sem, plane_sem) = scratch[23:]
    me = lax.axis_index("wave")
    lev = lax.axis_index("lev")

    inputs = [
        pltpu.make_async_copy(spec_in, spec, in_sem.at[0]),
        pltpu.make_async_copy(waves_in, waves, in_sem.at[1]),
    ]
    for c in inputs:
        c.start()
    loads = [
        pltpu.make_async_copy(
            leg.at[pl.ds(256 * q, 256)], table.at[pl.ds(256 * q, 256)], table_sem.at[q]
        )
        for q in range(10)
    ]
    for c in loads:
        c.start()

    barrier = pltpu.get_barrier_semaphore()

    def greet(d, _):
        pl.semaphore_signal(
            barrier, inc=1, device_id=(lax.rem(me + d, SETS), lev), device_id_type=MESH
        )
        return 0

    z_peers = sorted({o % LEVELS for n in NEAR + [HOP] for o in (n, -n)})
    for d in z_peers:
        pl.semaphore_signal(
            barrier, inc=1, device_id=(me, lax.rem(lev + d, LEVELS)), device_id_type=MESH
        )
    lax.fori_loop(1, SETS, greet, 0)

    for c in inputs:
        c.wait()
    m_lane = jnp.concatenate([waves[...].astype(F32)] * 4, axis=1)
    m_sub = jnp.broadcast_to(m_lane, (LANES, LANES)).T
    lane8 = lax.broadcasted_iota(jnp.int32, (8, LANES), 1)
    own_m = jnp.sum(jnp.where(lane8[0:1, 0:SETS] == me, m_lane[:, 0:SETS], 0.0), axis=1, keepdims=True)
    degree = lax.broadcasted_iota(jnp.int32, (4, DEG), 1).astype(F32)
    kept = degree <= (DEG - 1.0) - own_m
    rows = jnp.concatenate([spec[0].astype(F32), spec[1].astype(F32)], axis=0)
    rows = jnp.where(kept, rows, 0.0)
    own_s[...] = rows[2:4].astype(BF16)
    group_of = lane8 // 8
    group_masks = [group_of == g for g in range(16)]

    def eight(x):
        pad = jnp.zeros((8 - x.shape[0], DEG), F32)
        return jnp.concatenate([x, pad], axis=0).astype(BF16)

    def product(left, q):
        nat_s[:, 256 * q : 256 * q + 256] = lax.dot_general(
            left,
            table[256 * q : 256 * q + 256, :],
            (((1,), (1,)), ((), ())),
            preferred_element_type=F32,
        )

    def post(stage):
        for w in range(SETS):
            acc = None
            for q in range(10):
                chunk = w if q < 5 else SETS - 1 - w
                at = 256 * q + LANES * (chunk // 16)
                shift = (8 * q - 8 * (chunk % 16)) % LANES
                piece = nat_s[:, at : at + LANES]
                piece = pltpu.roll(piece, shift, 1) if shift else piece
                acc = piece if acc is None else jnp.where(group_masks[q], piece, acc)
            sends[stage, w] = acc.astype(BF16)

    def plane_copy(stage, d):
        to = lax.rem(me + d, SETS)
        return pltpu.make_async_remote_copy(
            src_ref=sends.at[stage, to],
            dst_ref=gets.at[stage, me],
            send_sem=plane_sem.at[stage, 0, d],
            recv_sem=plane_sem.at[stage, 1, d],
            device_id=(to, lev),
            device_id_type=MESH,
        )

    def plane_start(stage):
        def one(d, _):
            plane_copy(stage, d).start()
            return 0

        lax.fori_loop(1, SETS, one, 0, unroll=True)
        gets[stage, me] = sends[stage, me]

    def plane_wait(stage):
        def one(d, _):
            origin = lax.rem(me - d + SETS, SETS)
            pltpu.make_async_remote_copy(
                src_ref=sends.at[stage, lax.rem(me + d, SETS)],
                dst_ref=gets.at[stage, origin],
                send_sem=plane_sem.at[stage, 0, d],
                recv_sem=plane_sem.at[stage, 1, d],
                device_id=(origin, lev),
                device_id_type=MESH,
            ).wait()
            return 0

        lax.fori_loop(1, SETS, one, 0, unroll=True)

    def z_copy(src, dst, sems, i, shift):
        return pltpu.make_async_remote_copy(
            src_ref=src,
            dst_ref=dst,
            send_sem=sems.at[0, i],
            recv_sem=sems.at[1, i],
            device_id=(me, lax.rem(lev + shift, LEVELS)),
            device_id_type=MESH,
        )

    nears = [
        z_copy(own_s, near_s.at[i], near_sem, i, (-o) % LEVELS) for i, o in enumerate(NEAR)
    ]
    rights = [
        z_copy(node_s if s == 0 else right_s.at[s - 1], right_s.at[s], right_sem, s, HOP)
        for s in range(RIGHT)
    ]
    lefts = [
        z_copy(node_s if s == 0 else left_s.at[s - 1], left_s.at[s], left_sem, s, LEVELS - HOP)
        for s in range(LEFT)
    ]

    def ring(s):
        if s < RIGHT:
            rights[s].wait_recv()
            if s + 1 < RIGHT:
                rights[s + 1].start()
            total_s[...] += right_s[s].astype(F32)
        if s < LEFT:
            lefts[s].wait_recv()
            if s + 1 < LEFT:
                lefts[s + 1].start()
            total_s[...] += left_s[s].astype(F32)

    t_lane = lax.broadcasted_iota(jnp.int32, (64, LANES), 1).astype(F32)

    def tables(q):
        a_sub = lax.broadcasted_iota(jnp.int32, (ROWS[q], LANES), 0)
        lane = lax.broadcasted_iota(jnp.int32, (ROWS[q], LANES), 1)
        coarse_base = (a_sub * LANES).astype(F32) * m_lane
        coarse_shift = jnp.where(lane < 64, 0.0, 0.25)
        fine_base = m_sub[0:64] * t_lane
        fine_shift = jnp.where(lax.broadcasted_iota(jnp.int32, (64, LANES), 0) < SETS, 0.0, 0.25)

        def one(r, _):
            n = 8 * q + r
            j = 256 * q + 8 * me + r
            length = jnp.full((8, LANES), 20 + 4 * j, jnp.int32).astype(F32)
            inv = 1.0 / length
            turn = (jnp.full((8, LANES), j, jnp.int32).astype(F32) + 0.5) / 5120.0
            planet = 2.0 * cos_turns(turn)
            weight = cos_turns(turn - 0.25) * lax.rsqrt(length)
            pair_s[n, 0] = planet
            pair_s[n, 1] = weight
            length, inv = length[0:1], inv[0:1]
            fine = cos_turns(turns(fine_base, inv, length) + fine_shift).astype(BF16)
            fine_s[n, 0:64] = fine
            fine_s[n, 64:128] = fine
            coarse_s[q][r] = cos_turns(turns(coarse_base, inv, length) - coarse_shift)
            return 0

        lax.fori_loop(0, 8, one, 0, unroll=2)

    scale = 1.0 / math.sqrt(LEVELS)

    def take_lines(stage, count, base):
        wide[...] = gets[stage].astype(F32).reshape(SETS * 8, LANES)
        for k in range(count):
            re = wide[pl.ds(2 * k, SETS, stride=8), :] * scale
            im = wide[pl.ds(2 * k + 1, SETS, stride=8), :] * scale
            lines[base + k] = jnp.concatenate([re, im, -im, re], axis=0).T

    def shown(x, inside):
        count = x.shape[0]
        tail = jnp.where(inside, x[count - 16 :], 0.0)
        return tail if count == 16 else jnp.concatenate([x[: count - 16], tail], axis=0)

    def analyse(field, parts, n, coarse, fine, weight):
        count = coarse.shape[0]
        tend = jnp.concatenate(parts, axis=0).astype(BF16)
        back = lax.dot_general(tend, fine, (((1,), (1,)), ((), ())), preferred_element_type=F32)
        for h, at in enumerate((n, 79 - n)):
            line = jnp.sum(back[h * count : (h + 1) * count] * coarse, axis=0, keepdims=True)
            sums[field, pl.ds(at, 1), :] = line * weight

    def synth(q):
        count = ROWS[q]
        a_sub = lax.broadcasted_iota(jnp.int32, (16, LANES), 0) + (count - 16)
        point = a_sub * LANES + lax.broadcasted_iota(jnp.int32, (16, LANES), 1)

        def one(r, _):
            n = 8 * q + r
            j = 256 * q + 8 * me + r
            coarse = coarse_s[q][r]
            fine = fine_s[n]
            planet = pair_s[n, 0, 0:1]
            parts = [
                lines[k, pl.ds(at, 1), :] * coarse for k in range(2) for at in (n, 79 - n)
            ]
            left = jnp.concatenate(parts, axis=0).astype(BF16)
            grid = jnp.dot(left, fine, preferred_element_type=F32)
            inside = point < (20 + 4 * j)
            first = []
            for h, sign in ((0, 1.0), (1, -1.0)):
                vort = grid[h * count : (h + 1) * count]
                div = shown(grid[(2 + h) * count : (3 + h) * count], inside)
                total = vort + sign * planet
                first.append(total * div)
                grid_s[q][r, h * count : (h + 1) * count] = shown(total * vort, inside)
                grid_s[q][r, (2 + h) * count : (3 + h) * count] = div
            analyse(0, first, n, coarse, fine, -pair_s[n, 1, 0:1])
            return 0

        lax.fori_loop(0, 8, one, 0, unroll=2)

    def finish(q):
        count = ROWS[q]

        def one(r, _):
            n = 8 * q + r
            coarse = coarse_s[q][r]
            fine = fine_s[n]
            left = jnp.concatenate(
                [lines[2, pl.ds(at, 1), :] * coarse for at in (n, 79 - n)], axis=0
            ).astype(BF16)
            col = jnp.dot(left, fine, preferred_element_type=F32)
            second = grid_s[q][r, 0 : 2 * count] - grid_s[q][r, 2 * count : 4 * count] * col
            analyse(1, [second], n, coarse, fine, pair_s[n, 1, 0:1])
            return 0

        lax.fori_loop(0, 8, one, 0, unroll=FINISH)

    own = eight(rows)
    sums[...] = jnp.zeros_like(sums)
    pl.semaphore_wait(barrier, SETS - 1 + len(z_peers))
    for c in nears:
        c.start()

    def products(low, high):
        for q in range(low, high):
            loads[q].wait()
            product(own, q)

    def launch():
        node = rows[2:4]
        for i, c in enumerate(nears):
            c.wait_recv()
            node += near_s[i].astype(F32)
        node_s[...] = node.astype(BF16)
        total_s[...] = node_s[...].astype(F32)
        rights[0].start()
        lefts[0].start()

    def collect():
        plane_wait(0)
        take_lines(0, 2, 0)

    def send_own():
        plane_start(0)
        tables(0)

    work = [
        lambda: products(5, 8),
        lambda: (products(8, 10), post(0)),
        send_own,
        lambda: tables(1),
        lambda: tables(2),
        lambda: tables(3),
        lambda: tables(4),
        collect,
        lambda: synth(0),
        lambda: synth(1),
        lambda: synth(2),
        lambda: synth(3),
        lambda: synth(4),
    ]
    products(0, 5)
    launch()
    done = 0
    for i, item in enumerate(work):
        item()
        while done < (i + 1) * RIGHT // (len(work) + 1):
            ring(done)
            done += 1
    for s in range(done, RIGHT):
        ring(s)
    total = total_s[...]
    column = eight(total * scale)
    for q in range(10):
        product(column, q)
    post(1)
    for c in nears + rights + lefts:
        c.wait_send()
    plane_start(1)
    plane_wait(1)
    take_lines(1, 1, 2)
    for q in range(5):
        finish(q)
    for k in range(2):
        cols = sums[k].T
        wide[pl.ds(2 * k, SETS, stride=8), :] = cols[0:32] + cols[96:128]
        wide[pl.ds(2 * k + 1, SETS, stride=8), :] = cols[32:64] - cols[64:96]
        wide[pl.ds(2 * k + 4, SETS, stride=8), :] = jnp.zeros((SETS, LANES), F32)
        wide[pl.ds(2 * k + 5, SETS, stride=8), :] = jnp.zeros((SETS, LANES), F32)
    sends[2] = wide[...].reshape(SETS, 8, LANES).astype(BF16)
    plane_start(2)
    plane_wait(2)
    wide[...] = gets[2].astype(F32).reshape(SETS * 8, LANES)
    result = jnp.zeros((8, DEG), F32)
    for q in range(10):
        halves = []
        for b in range(2):
            acc = None
            for g in range(16):
                w = 16 * b + g
                w = w if q < 5 else SETS - 1 - w
                shift = (8 * g - 8 * q) % LANES
                piece = wide[8 * w : 8 * w + 8, :]
                piece = pltpu.roll(piece, shift, 1) if shift else piece
                acc = piece if acc is None else jnp.where(group_masks[g], piece, acc)
            halves.append(acc)
        left = jnp.concatenate(halves, axis=1).astype(BF16)
        result += jnp.dot(
            left, table[256 * q : 256 * q + 256, :], preferred_element_type=F32
        )
    result = result[0:4]
    result = jnp.where(kept, result, 0.0)
    out[0] = result[0:2].astype(BF16)
    out[1] = result[2:4].astype(BF16)


def body(spectral, legendre, wavenumber):
    anywhere = pl.BlockSpec(memory_space=pl.ANY)
    local = pl.BlockSpec(memory_space=pltpu.VMEM)
    dma = pltpu.SemaphoreType.DMA
    scratch = [
        pltpu.VMEM((2, 2, DEG), BF16),
        pltpu.VMEM((1, SETS), jnp.int32),
        dma((2,)),
        pltpu.VMEM((LATS, DEG), BF16),
        dma((10,)),
        pltpu.VMEM((3, SETS, 8, LANES), BF16),
        pltpu.VMEM((3, SETS, 8, LANES), BF16),
        pltpu.VMEM((SETS * 8, LANES), F32),
        pltpu.VMEM((3, LANES, LANES), F32),
        pltpu.VMEM((2, LANES, LANES), F32),
        pltpu.VMEM((40, LANES, LANES), BF16),
        pltpu.VMEM((40, 2, 8, LANES), F32),
        pltpu.VMEM((8, LATS), F32),
    ]
    scratch += [pltpu.VMEM((8, n, LANES), F32) for n in ROWS]
    scratch += [pltpu.VMEM((8, 4 * n, LANES), F32) for n in ROWS]
    scratch += [
        pltpu.VMEM((2, DEG), BF16),
        pltpu.VMEM((max(len(NEAR), 1), 2, DEG), BF16),
        pltpu.VMEM((2, DEG), BF16),
        pltpu.VMEM((2, DEG), F32),
        pltpu.VMEM((RIGHT, 2, DEG), BF16),
        pltpu.VMEM((LEFT, 2, DEG), BF16),
        dma((2, max(len(NEAR), 1))),
        dma((2, RIGHT)),
        dma((2, LEFT)),
        dma((3, 2, SETS)),
    ]
    result = pl.pallas_call(
        kernel,
        out_shape=jax.ShapeDtypeStruct((2, 2, DEG), BF16),
        in_specs=[anywhere, anywhere, anywhere],
        out_specs=local,
        scratch_shapes=scratch,
        compiler_params=pltpu.CompilerParams(
            collective_id=0, has_side_effects=True, vmem_limit_bytes=62_000_000
        ),
    )(spectral.reshape(2, 2, DEG), wavenumber.reshape(1, SETS), legendre.reshape(LATS, DEG))
    return result.reshape(2, 1, 2, 1, DEG)


def solution(mesh):
    in_specs = (P(None, "lev", None, "wave", None), P("wave", None, None), P())
    out_specs = P(None, "lev", None, "wave", None)
    return jax.shard_map(body, mesh=mesh, in_specs=in_specs, out_specs=out_specs, check_vma=False)
```

time: 76.7 us -> 64.7 us (0.84)
  Pallas kernels: 74.6 us -> 63.2 us
    pallas_call x1, Pallas kernels: 74.6 us -> 63.2 us  [body(): pl.pallas_call(kernel, out_shape=jax.ShapeDtypeStruct((2, 2, DEG), BF16),...]
    unnamed x5 -> x1, local copies, waits for them, and re-layouts: 1.96 us -> 1.31 us
where the time goes in v3:
time: 64.7 us; the launch traced here: 64.5 us
  Pallas kernels  63.2 us (98%)
  local copies, waits for them, and re-layouts  1.31 us (2%)
    pallas_call x1, Pallas kernels, body(): pl.pallas_call(kernel, out_shape=jax.ShapeDtypeStruct((2, 2, DEG), BF16),...  63.2 us
    unnamed x1, local copies, waits for them, and re-layouts  1.31 us

profile of v3, /device:TPU:1, one launch (start us, length us, event | category | flops | bytes accessed | tf_op | source)
XLA Modules:
  0.0 64.5 jit_solution(4466639462075866918)
XLA Ops:
  0.0 63.2 %shard_map.37 = bf16[2,2,1280]{2,1,0:T(2,128)(2,1)} custom-call(bf16[2,2,1280]{2,1,0:T(2,128)(2,1)} %bitcast.8, s32[1,32]{1,0:T(1,128)} %bitcast.9, bf16[2560,1280]{1,0:T(8,128)(2,1)} %bitcast.6), custom_call_target="tpu_custom_call" | custom-call | tf_op jit(solution)/shard_map/pallas_call | solution.py:419
  63.2 1.3 %copy.6 = bf16[2,1,2,1,1280]{4,2,3,1,0:T(2,128)(2,1)} copy(bf16[2,1,2,1,1280]{4,2,3,1,0:T(2,128)(2,1)} %bitcast.7) | data formatting | bytes 20480

commit v4 on v3

--- a/solution.py
+++ b/solution.py
@@ -13,11 +13,9 @@
 SETS = 32
 LEVELS = 32
 LANES = 128
-HOP = 8
-NODES = LEVELS // HOP
-RIGHT = NODES // 2
-NEAR = [o for o in range(1 - HOP // 2, HOP // 2 + 1) if o] if HOP > 1 else []
-LEFT = NODES - 1 - RIGHT
+REACH = 5
+SPAN = 2 * REACH + 1
+NEAR = [o * side for o in range(REACH, 0, -1) for side in (1, -1)]
 FINISH = 4
 ROWS = (16, 24, 32, 40, 48)
 F32 = jnp.float32
@@ -46,7 +44,7 @@
     (spec, waves, in_sem, table, table_sem, sends, gets, wide, lines, sums, fine_s, pair_s, nat_s) = scratch[:13]
     coarse_s = scratch[13:18]
     grid_s = scratch[18:23]
-    (own_s, near_s, node_s, total_s, right_s, left_s, near_sem, right_sem, left_sem, plane_sem) = scratch[23:]
+    (own_s, near_s, node_s, far_s, near_sem, far_sem, plane_sem) = scratch[23:]
     me = lax.axis_index("wave")
     lev = lax.axis_index("lev")
 
@@ -73,7 +71,7 @@
         )
         return 0
 
-    z_peers = sorted({o % LEVELS for n in NEAR + [HOP] for o in (n, -n)})
+    z_peers = [o % LEVELS for o in range(-REACH - 1, REACH + 2) if o]
     for d in z_peers:
         pl.semaphore_signal(
             barrier, inc=1, device_id=(me, lax.rem(lev + d, LEVELS)), device_id_type=MESH
@@ -137,17 +135,18 @@
         lax.fori_loop(1, SETS, one, 0, unroll=True)
         gets[stage, me] = sends[stage, me]
 
-    def plane_wait(stage):
+    def plane_wait(stage, sent=False):
         def one(d, _):
             origin = lax.rem(me - d + SETS, SETS)
-            pltpu.make_async_remote_copy(
+            copy = pltpu.make_async_remote_copy(
                 src_ref=sends.at[stage, lax.rem(me + d, SETS)],
                 dst_ref=gets.at[stage, origin],
                 send_sem=plane_sem.at[stage, 0, d],
                 recv_sem=plane_sem.at[stage, 1, d],
                 device_id=(origin, lev),
                 device_id_type=MESH,
-            ).wait()
+            )
+            copy.wait_send() if sent else copy.wait_recv()
             return 0
 
         lax.fori_loop(1, SETS, one, 0, unroll=True)
@@ -165,26 +164,10 @@
     nears = [
         z_copy(own_s, near_s.at[i], near_sem, i, (-o) % LEVELS) for i, o in enumerate(NEAR)
     ]
-    rights = [
-        z_copy(node_s if s == 0 else right_s.at[s - 1], right_s.at[s], right_sem, s, HOP)
-        for s in range(RIGHT)
-    ]
-    lefts = [
-        z_copy(node_s if s == 0 else left_s.at[s - 1], left_s.at[s], left_sem, s, LEVELS - HOP)
-        for s in range(LEFT)
-    ]
-
-    def ring(s):
-        if s < RIGHT:
-            rights[s].wait_recv()
-            if s + 1 < RIGHT:
-                rights[s + 1].start()
-            total_s[...] += right_s[s].astype(F32)
-        if s < LEFT:
-            lefts[s].wait_recv()
-            if s + 1 < LEFT:
-                lefts[s + 1].start()
-            total_s[...] += left_s[s].astype(F32)
+    fars = [
+        z_copy(node_s.at[i], far_s.at[i], far_sem, i, shift)
+        for i, shift in enumerate((LEVELS - SPAN, SPAN))
+    ]
 
     t_lane = lax.broadcasted_iota(jnp.int32, (64, LANES), 1).astype(F32)
 
@@ -297,54 +280,39 @@
 
     def launch():
         node = rows[2:4]
+        last = None
         for i, c in enumerate(nears):
             c.wait_recv()
-            node += near_s[i].astype(F32)
-        node_s[...] = node.astype(BF16)
-        total_s[...] = node_s[...].astype(F32)
-        rights[0].start()
-        lefts[0].start()
-
-    def collect():
-        plane_wait(0)
-        take_lines(0, 2, 0)
-
-    def send_own():
-        plane_start(0)
-        tables(0)
-
-    work = [
-        lambda: products(5, 8),
-        lambda: (products(8, 10), post(0)),
-        send_own,
-        lambda: tables(1),
-        lambda: tables(2),
-        lambda: tables(3),
-        lambda: tables(4),
-        collect,
-        lambda: synth(0),
-        lambda: synth(1),
-        lambda: synth(2),
-        lambda: synth(3),
-        lambda: synth(4),
-    ]
-    products(0, 5)
+            term = near_s[i].astype(F32)
+            if NEAR[i] == -REACH:
+                last = term
+            else:
+                node += term
+        node_s[0] = (node + last).astype(BF16)
+        node_s[1] = node.astype(BF16)
+
+    products(0, 10)
+    post(0)
+    tables(0)
+    plane_start(0)
     launch()
-    done = 0
-    for i, item in enumerate(work):
-        item()
-        while done < (i + 1) * RIGHT // (len(work) + 1):
-            ring(done)
-            done += 1
-    for s in range(done, RIGHT):
-        ring(s)
-    total = total_s[...]
+    tables(1)
+    for c in fars:
+        c.start()
+    for q in range(2, 5):
+        tables(q)
+    plane_wait(0)
+    take_lines(0, 2, 0)
+    for q in range(5):
+        synth(q)
+    total = node_s[0].astype(F32)
+    for i, c in enumerate(fars):
+        c.wait_recv()
+        total += far_s[i].astype(F32)
     column = eight(total * scale)
     for q in range(10):
         product(column, q)
     post(1)
-    for c in nears + rights + lefts:
-        c.wait_send()
     plane_start(1)
     plane_wait(1)
     take_lines(1, 1, 2)
@@ -377,6 +345,10 @@
         result += jnp.dot(
             left, table[256 * q : 256 * q + 256, :], preferred_element_type=F32
         )
+    for c in nears + fars:
+        c.wait_send()
+    for stage in range(3):
+        plane_wait(stage, sent=True)
     result = result[0:4]
     result = jnp.where(kept, result, 0.0)
     out[0] = result[0:2].astype(BF16)
@@ -406,14 +378,11 @@
     scratch += [pltpu.VMEM((8, 4 * n, LANES), F32) for n in ROWS]
     scratch += [
         pltpu.VMEM((2, DEG), BF16),
-        pltpu.VMEM((max(len(NEAR), 1), 2, DEG), BF16),
-        pltpu.VMEM((2, DEG), BF16),
-        pltpu.VMEM((2, DEG), F32),
-        pltpu.VMEM((RIGHT, 2, DEG), BF16),
-        pltpu.VMEM((LEFT, 2, DEG), BF16),
-        dma((2, max(len(NEAR), 1))),
-        dma((2, RIGHT)),
-        dma((2, LEFT)),
+        pltpu.VMEM((len(NEAR), 2, DEG), BF16),
+        pltpu.VMEM((2, 2, DEG), BF16),
+        pltpu.VMEM((2, 2, DEG), BF16),
+        dma((2, len(NEAR))),
+        dma((2, 2)),
         dma((3, 2, SETS)),
     ]
     result = pl.pallas_call(

time: 64.7 us -> 61.9 us (0.957)
  Pallas kernels: 63.2 us -> 60.3 us
    pallas_call x1, Pallas kernels: 63.2 us -> 60.3 us  [body(): pl.pallas_call(kernel, out_shape=jax.ShapeDtypeStruct((2, 2, DEG), BF16),...]
where the time goes in v4:
time: 61.9 us; the launch traced here: 61.7 us
  Pallas kernels  60.3 us (97%)
  local copies, waits for them, and re-layouts  1.31 us (2%)
    pallas_call x1, Pallas kernels, body(): pl.pallas_call(kernel, out_shape=jax.ShapeDtypeStruct((2, 2, DEG), BF16),...  60.3 us
    unnamed x1, local copies, waits for them, and re-layouts  1.31 us

profile of v4, /device:TPU:1, one launch (start us, length us, event | category | flops | bytes accessed | tf_op | source)
XLA Modules:
  0.0 61.7 jit_solution(13718853611411567963)
XLA Ops:
  0.0 60.3 %shard_map.37 = bf16[2,2,1280]{2,1,0:T(2,128)(2,1)} custom-call(bf16[2,2,1280]{2,1,0:T(2,128)(2,1)} %bitcast.8, s32[1,32]{1,0:T(1,128)} %bitcast.9, bf16[2560,1280]{1,0:T(8,128)(2,1)} %bitcast.6), custom_call_target="tpu_custom_call" | custom-call | tf_op jit(solution)/shard_map/pallas_call | solution.py:388
  60.4 1.3 %copy.6 = bf16[2,1,2,1,1280]{4,2,3,1,0:T(2,128)(2,1)} copy(bf16[2,1,2,1,1280]{4,2,3,1,0:T(2,128)(2,1)} %bitcast.7) | data formatting | bytes 20480

commit v5 on v4

--- a/solution.py
+++ b/solution.py
@@ -17,6 +17,11 @@
 SPAN = 2 * REACH + 1
 NEAR = [o * side for o in range(REACH, 0, -1) for side in (1, -1)]
 FINISH = 4
+HALVES = (((0, 1, 2), (0, 1, 2, 7, 8, 9)), ((3, 4), (3, 4, 5, 6)))
+PEERS = sorted(
+    ((dx, dy, dc) for dx in range(4) for dy in range(4) for dc in range(2) if dx + dy + dc),
+    key=lambda p: -(min(p[0], 4 - p[0]) + min(p[1], 4 - p[1])),
+)
 ROWS = (16, 24, 32, 40, 48)
 F32 = jnp.float32
 BF16 = jnp.bfloat16
@@ -41,10 +46,10 @@
 
 
 def kernel(spec_in, waves_in, leg, out, *scratch):
-    (spec, waves, in_sem, table, table_sem, sends, gets, wide, lines, sums, fine_s, pair_s, nat_s) = scratch[:13]
-    coarse_s = scratch[13:18]
-    grid_s = scratch[18:23]
-    (own_s, near_s, node_s, far_s, near_sem, far_sem, plane_sem) = scratch[23:]
+    (spec, waves, in_sem, table, table_sem, sends, gets, wide, back_s, lines, sums, fine_s, pair_s, nat_s) = scratch[:14]
+    coarse_s = scratch[14:19]
+    grid_s = scratch[19:24]
+    (own_s, near_s, node_s, far_s, near_sem, far_sem, plane_sem) = scratch[24:]
     me = lax.axis_index("wave")
     lev = lax.axis_index("lev")
 
@@ -104,10 +109,10 @@
             preferred_element_type=F32,
         )
 
-    def post(stage):
+    def post(stage, chunks):
         for w in range(SETS):
             acc = None
-            for q in range(10):
+            for q in chunks:
                 chunk = w if q < 5 else SETS - 1 - w
                 at = 256 * q + LANES * (chunk // 16)
                 shift = (8 * q - 8 * (chunk % 16)) % LANES
@@ -116,40 +121,38 @@
                 acc = piece if acc is None else jnp.where(group_masks[q], piece, acc)
             sends[stage, w] = acc.astype(BF16)
 
-    def plane_copy(stage, d):
-        to = lax.rem(me + d, SETS)
+    def parts(sign):
+        x, y, c = me // 8, (me // 2) % 4, me % 2
+        return (
+            [(x + sign * d + 4) % 4 * 8 for d in range(4)],
+            [(y + sign * d + 4) % 4 * 2 for d in range(4)],
+            [(c + d) % 2 for d in range(2)],
+        )
+
+    ahead, behind = parts(1), parts(-1)
+
+    def plane_copy(stage, i, receive):
+        dx, dy, dc = PEERS[i]
+        to = ahead[0][dx] + ahead[1][dy] + ahead[2][dc]
+        origin = behind[0][dx] + behind[1][dy] + behind[2][dc]
         return pltpu.make_async_remote_copy(
             src_ref=sends.at[stage, to],
-            dst_ref=gets.at[stage, me],
-            send_sem=plane_sem.at[stage, 0, d],
-            recv_sem=plane_sem.at[stage, 1, d],
+            dst_ref=gets.at[stage, origin if receive else me],
+            send_sem=plane_sem.at[stage, 0, i],
+            recv_sem=plane_sem.at[stage, 1, i],
             device_id=(to, lev),
             device_id_type=MESH,
         )
 
     def plane_start(stage):
-        def one(d, _):
-            plane_copy(stage, d).start()
-            return 0
-
-        lax.fori_loop(1, SETS, one, 0, unroll=True)
+        for i in range(len(PEERS)):
+            plane_copy(stage, i, False).start()
         gets[stage, me] = sends[stage, me]
 
     def plane_wait(stage, sent=False):
-        def one(d, _):
-            origin = lax.rem(me - d + SETS, SETS)
-            copy = pltpu.make_async_remote_copy(
-                src_ref=sends.at[stage, lax.rem(me + d, SETS)],
-                dst_ref=gets.at[stage, origin],
-                send_sem=plane_sem.at[stage, 0, d],
-                recv_sem=plane_sem.at[stage, 1, d],
-                device_id=(origin, lev),
-                device_id_type=MESH,
-            )
+        for i in range(len(PEERS)):
+            copy = plane_copy(stage, i, True)
             copy.wait_send() if sent else copy.wait_recv()
-            return 0
-
-        lax.fori_loop(1, SETS, one, 0, unroll=True)
 
     def z_copy(src, dst, sems, i, shift):
         return pltpu.make_async_remote_copy(
@@ -267,7 +270,13 @@
 
         lax.fori_loop(0, 8, one, 0, unroll=FINISH)
 
+    def spread(k):
+        cols = sums[k].T
+        back_s[pl.ds(2 * k, SETS, stride=8), :] = cols[0:32] + cols[96:128]
+        back_s[pl.ds(2 * k + 1, SETS, stride=8), :] = cols[32:64] - cols[64:96]
+
     own = eight(rows)
+    back_s[...] = jnp.zeros_like(back_s)
     sums[...] = jnp.zeros_like(sums)
     pl.semaphore_wait(barrier, SETS - 1 + len(z_peers))
     for c in nears:
@@ -292,7 +301,7 @@
         node_s[1] = node.astype(BF16)
 
     products(0, 10)
-    post(0)
+    post(0, range(10))
     tables(0)
     plane_start(0)
     launch()
@@ -305,50 +314,50 @@
     take_lines(0, 2, 0)
     for q in range(5):
         synth(q)
+    spread(0)
     total = node_s[0].astype(F32)
     for i, c in enumerate(fars):
         c.wait_recv()
         total += far_s[i].astype(F32)
     column = eight(total * scale)
-    for q in range(10):
-        product(column, q)
-    post(1)
-    plane_start(1)
-    plane_wait(1)
-    take_lines(1, 1, 2)
-    for q in range(5):
-        finish(q)
-    for k in range(2):
-        cols = sums[k].T
-        wide[pl.ds(2 * k, SETS, stride=8), :] = cols[0:32] + cols[96:128]
-        wide[pl.ds(2 * k + 1, SETS, stride=8), :] = cols[32:64] - cols[64:96]
-        wide[pl.ds(2 * k + 4, SETS, stride=8), :] = jnp.zeros((SETS, LANES), F32)
-        wide[pl.ds(2 * k + 5, SETS, stride=8), :] = jnp.zeros((SETS, LANES), F32)
-    sends[2] = wide[...].reshape(SETS, 8, LANES).astype(BF16)
-    plane_start(2)
-    plane_wait(2)
-    wide[...] = gets[2].astype(F32).reshape(SETS * 8, LANES)
-    result = jnp.zeros((8, DEG), F32)
-    for q in range(10):
-        halves = []
-        for b in range(2):
-            acc = None
-            for g in range(16):
-                w = 16 * b + g
-                w = w if q < 5 else SETS - 1 - w
-                shift = (8 * g - 8 * q) % LANES
-                piece = wide[8 * w : 8 * w + 8, :]
-                piece = pltpu.roll(piece, shift, 1) if shift else piece
-                acc = piece if acc is None else jnp.where(group_masks[g], piece, acc)
-            halves.append(acc)
-        left = jnp.concatenate(halves, axis=1).astype(BF16)
-        result += jnp.dot(
-            left, table[256 * q : 256 * q + 256, :], preferred_element_type=F32
-        )
+    for half, (_, chunks) in enumerate(HALVES):
+        for q in chunks:
+            product(column, q)
+        post(1 + half, chunks)
+        plane_start(1 + half)
+    for half, (own_lats, _) in enumerate(HALVES):
+        plane_wait(1 + half)
+        take_lines(1 + half, 1, 2)
+        for q in own_lats:
+            finish(q)
+        spread(1)
+        sends[3 + half] = back_s[...].reshape(SETS, 8, LANES).astype(BF16)
+        plane_start(3 + half)
     for c in nears + fars:
         c.wait_send()
     for stage in range(3):
         plane_wait(stage, sent=True)
+    result = jnp.zeros((8, DEG), F32)
+    for half, (_, chunks) in enumerate(HALVES):
+        plane_wait(3 + half, sent=True)
+        plane_wait(3 + half)
+        wide[...] = gets[3 + half].astype(F32).reshape(SETS * 8, LANES)
+        for q in chunks:
+            halves = []
+            for b in range(2):
+                acc = None
+                for g in range(16):
+                    w = 16 * b + g
+                    w = w if q < 5 else SETS - 1 - w
+                    shift = (8 * g - 8 * q) % LANES
+                    piece = wide[8 * w : 8 * w + 8, :]
+                    piece = pltpu.roll(piece, shift, 1) if shift else piece
+                    acc = piece if acc is None else jnp.where(group_masks[g], piece, acc)
+                halves.append(acc)
+            left = jnp.concatenate(halves, axis=1).astype(BF16)
+            result += jnp.dot(
+                left, table[256 * q : 256 * q + 256, :], preferred_element_type=F32
+            )
     result = result[0:4]
     result = jnp.where(kept, result, 0.0)
     out[0] = result[0:2].astype(BF16)
@@ -365,8 +374,9 @@
         dma((2,)),
         pltpu.VMEM((LATS, DEG), BF16),
         dma((10,)),
-        pltpu.VMEM((3, SETS, 8, LANES), BF16),
-        pltpu.VMEM((3, SETS, 8, LANES), BF16),
+        pltpu.VMEM((5, SETS, 8, LANES), BF16),
+        pltpu.VMEM((5, SETS, 8, LANES), BF16),
+        pltpu.VMEM((SETS * 8, LANES), F32),
         pltpu.VMEM((SETS * 8, LANES), F32),
         pltpu.VMEM((3, LANES, LANES), F32),
         pltpu.VMEM((2, LANES, LANES), F32),
@@ -383,7 +393,7 @@
         pltpu.VMEM((2, 2, DEG), BF16),
         dma((2, len(NEAR))),
         dma((2, 2)),
-        dma((3, 2, SETS)),
+        dma((5, 2, SETS)),
     ]
     result = pl.pallas_call(
         kernel,

time: 61.9 us -> 61.7 us (level)
  no operation moved by 1% of the time
where the time goes in v5:
time: 61.7 us; the launch traced here: 61.5 us
  Pallas kernels  60.2 us (98%)
  local copies, waits for them, and re-layouts  1.31 us (2%)
    pallas_call x1, Pallas kernels, body(): pl.pallas_call(kernel, out_shape=jax.ShapeDtypeStruct((2, 2, DEG), BF16),...  60.2 us
    unnamed x1, local copies, waits for them, and re-layouts  1.31 us

profile of v5, /device:TPU:1, one launch (start us, length us, event | category | flops | bytes accessed | tf_op | source)
XLA Modules:
  0.0 61.5 jit_solution(3018792444000986605)
XLA Ops:
  0.0 60.2 %shard_map.37 = bf16[2,2,1280]{2,1,0:T(2,128)(2,1)} custom-call(bf16[2,2,1280]{2,1,0:T(2,128)(2,1)} %bitcast.8, s32[1,32]{1,0:T(1,128)} %bitcast.9, bf16[2560,1280]{1,0:T(8,128)(2,1)} %bitcast.6), custom_call_target="tpu_custom_call" | custom-call | tf_op jit(solution)/shard_map/pallas_call | solution.py:398
  60.2 1.3 %copy.6 = bf16[2,1,2,1,1280]{4,2,3,1,0:T(2,128)(2,1)} copy(bf16[2,1,2,1,1280]{4,2,3,1,0:T(2,128)(2,1)} %bitcast.7) | data formatting | bytes 20480

commit v6 on v5

--- a/solution.py
+++ b/solution.py
@@ -70,18 +70,24 @@
 
     barrier = pltpu.get_barrier_semaphore()
 
-    def greet(d, _):
-        pl.semaphore_signal(
-            barrier, inc=1, device_id=(lax.rem(me + d, SETS), lev), device_id_type=MESH
-        )
-        return 0
+    def parts(sign):
+        x, y, c = me // 8, (me // 2) % 4, me % 2
+        return (
+            [(x + sign * d + 4) % 4 * 8 for d in range(4)],
+            [(y + sign * d + 4) % 4 * 2 for d in range(4)],
+            [(c + d) % 2 for d in range(2)],
+        )
+
+    ahead, behind = parts(1), parts(-1)
 
     z_peers = [o % LEVELS for o in range(-REACH - 1, REACH + 2) if o]
     for d in z_peers:
         pl.semaphore_signal(
             barrier, inc=1, device_id=(me, lax.rem(lev + d, LEVELS)), device_id_type=MESH
         )
-    lax.fori_loop(1, SETS, greet, 0)
+    for dx, dy, dc in PEERS:
+        to = ahead[0][dx] + ahead[1][dy] + ahead[2][dc]
+        pl.semaphore_signal(barrier, inc=1, device_id=(to, lev), device_id_type=MESH)
 
     for c in inputs:
         c.wait()
@@ -120,16 +126,6 @@
                 piece = pltpu.roll(piece, shift, 1) if shift else piece
                 acc = piece if acc is None else jnp.where(group_masks[q], piece, acc)
             sends[stage, w] = acc.astype(BF16)
-
-    def parts(sign):
-        x, y, c = me // 8, (me // 2) % 4, me % 2
-        return (
-            [(x + sign * d + 4) % 4 * 8 for d in range(4)],
-            [(y + sign * d + 4) % 4 * 2 for d in range(4)],
-            [(c + d) % 2 for d in range(2)],
-        )
-
-    ahead, behind = parts(1), parts(-1)
 
     def plane_copy(stage, i, receive):
         dx, dy, dc = PEERS[i]
@@ -276,8 +272,6 @@
         back_s[pl.ds(2 * k + 1, SETS, stride=8), :] = cols[32:64] - cols[64:96]
 
     own = eight(rows)
-    back_s[...] = jnp.zeros_like(back_s)
-    sums[...] = jnp.zeros_like(sums)
     pl.semaphore_wait(barrier, SETS - 1 + len(z_peers))
     for c in nears:
         c.start()
@@ -305,10 +299,11 @@
     tables(0)
     plane_start(0)
     launch()
-    tables(1)
+    back_s[...] = jnp.zeros_like(back_s)
+    sums[...] = jnp.zeros_like(sums)
     for c in fars:
         c.start()
-    for q in range(2, 5):
+    for q in range(1, 5):
         tables(q)
     plane_wait(0)
     take_lines(0, 2, 0)

time: 61.7 us -> 61.7 us (level)
  no operation moved by 1% of the time
where the time goes in v6:
time: 61.7 us; the launch traced here: 61.5 us
  Pallas kernels  60.2 us (98%)
  local copies, waits for them, and re-layouts  1.31 us (2%)
    pallas_call x1, Pallas kernels, body(): pl.pallas_call(kernel, out_shape=jax.ShapeDtypeStruct((2, 2, DEG), BF16),...  60.2 us
    unnamed x1, local copies, waits for them, and re-layouts  1.31 us

profile of v6, /device:TPU:1, one launch (start us, length us, event | category | flops | bytes accessed | tf_op | source)
XLA Modules:
  0.0 61.5 jit_solution(10491533018233633927)
XLA Ops:
  0.0 60.2 %shard_map.37 = bf16[2,2,1280]{2,1,0:T(2,128)(2,1)} custom-call(bf16[2,2,1280]{2,1,0:T(2,128)(2,1)} %bitcast.8, s32[1,32]{1,0:T(1,128)} %bitcast.9, bf16[2560,1280]{1,0:T(8,128)(2,1)} %bitcast.6), custom_call_target="tpu_custom_call" | custom-call | tf_op jit(solution)/shard_map/pallas_call | solution.py:393
  60.2 1.3 %copy.6 = bf16[2,1,2,1,1280]{4,2,3,1,0:T(2,128)(2,1)} copy(bf16[2,1,2,1,1280]{4,2,3,1,0:T(2,128)(2,1)} %bitcast.7) | data formatting | bytes 20480
